TPU v7x, 32 devices: a whole 2x2x4 slice. The times are simulated.
32 devices in a mesh: grp: 4 (over x, core), sub: 8 (over z, y).
Axes of the slice: x: 2, y: 2, z: 4, core: 2. Of those that a mesh axis runs over, the one named last changes fastest.
Arguments:
- shell_state: float32 [2, 48, 262144], P(None, None, ('grp', 'sub')), may hold values from -6 to 6
- source: bfloat16 [2, 256, 16, 768], P(None, ('grp', 'sub')), may hold values from -6 to 6
- knockdown: bfloat16 [256, 16, 768], P(('grp', 'sub')), may hold values from 0.29882812 to 3
- orient: int32 [256, 48], P(('grp', 'sub')), may hold values from 0 to 3
- active: int32 [256], P(('grp', 'sub')), may hold values from 24 to 48
- point_owner: int32 [256, 64], P(('grp', 'sub')), may hold values from 0 to 31, as said below
- owner_nodes: int32 [32, 32, 32], P(('grp', 'sub')), may hold values from -1 to 8191, as said below
Outputs:
- adjoint: float32 [2, 256, 16, 768], P(None, ('grp', 'sub'))
- shell_force: float32 [2, 48, 262144], P(None, None, ('grp', 'sub'))
Inputs may be any that keep to these rules, and one draw needn't show every extreme that they name: `point_owner`: within every block of boundary columns (see the steps), no owner appears more than 32 times, and in every draw one owner, the same for all blocks, appears exactly 32 times in each block. owner_nodes[o, d, r] is the local node of the column of block d with owner o that has r earlier such columns, and -1 for r at or beyond the count of such columns.
All inputs are finite; a program needn't handle non-finite values.
Results may differ from a plain program's by a relative error of at most 0.0003.
Values sent between devices are 32-bit elements; how exact they have to be, the bound alone decides.
No kernel may reach another device: no remote copies, remote signals or barrier semaphores. Data moves between devices by JAX's collectives and lax.ppermute only.
A program may use at most 64 MiB of HBM per device.

v0:
```python
import math
import jax
import jax.numpy as jnp
from jax import lax
from jax.sharding import PartitionSpec as P

SWEEPS = 3
STEPS = 2
FIBER_COND = 1.0
TRANSVERSE = 0.25
THROUGH = 0.15
MASS_SHARE = 0.05
CHEB_CENTER = 1.02
CHEB_HALF = 0.98


def face_mean(lower_side, upper_side):
    return jnp.where((lower_side > 0) & (upper_side > 0), 0.5 * (lower_side + upper_side), 0.0)


def flat_coeffs(knock_flat, orient, active, side_cells):
    sub_count, side_x, flat_width = knock_flat.shape
    ply_count = orient.shape[1]
    active_mask = (jnp.arange(ply_count)[None, :] < active[:, None]).astype(jnp.float32)
    ply_angle = orient.astype(jnp.float32) * (math.pi / 6.0)
    cos_square = jnp.cos(ply_angle) ** 2
    fiber_part = (FIBER_COND * cos_square + TRANSVERSE * (1.0 - cos_square)) * active_mask
    cross_part = (FIBER_COND * (1.0 - cos_square) + TRANSVERSE * cos_square) * active_mask
    fiber_flat = jnp.repeat(fiber_part, side_cells, axis=1)[:, None, :]
    cross_flat = jnp.repeat(cross_part, side_cells, axis=1)[:, None, :]
    mask_flat = jnp.repeat(active_mask, side_cells, axis=1)[:, None, :]
    along_x = knock_flat * fiber_flat
    along_y = knock_flat * cross_flat
    across_ply = knock_flat * (THROUGH * mask_flat)
    flat_place = jnp.arange(flat_width)
    y_place = (flat_place % side_cells)[None, None, :]
    ply_place = (flat_place // side_cells)[None, None, :]
    x_place = jnp.arange(side_x)[None, :, None]
    face_west = jnp.where(x_place == 0, 0.0, face_mean(jnp.roll(along_x, 1, axis=1), along_x))
    face_east = jnp.where(
        x_place == side_x - 1, 0.0, face_mean(along_x, jnp.roll(along_x, -1, axis=1))
    )
    face_south = jnp.where(y_place == 0, 0.0, face_mean(jnp.roll(along_y, 1, axis=2), along_y))
    face_north = jnp.where(
        y_place == side_cells - 1, 0.0, face_mean(along_y, jnp.roll(along_y, -1, axis=2))
    )
    face_below = jnp.where(
        ply_place == 0, 0.0, face_mean(jnp.roll(across_ply, side_cells, axis=2), across_ply)
    )
    face_above = jnp.where(
        ply_place == ply_count - 1,
        0.0,
        face_mean(across_ply, jnp.roll(across_ply, -side_cells, axis=2)),
    )
    ghost_west = jnp.where(x_place == 0, along_x, 0.0)
    ghost_east = jnp.where(x_place == side_x - 1, along_x, 0.0)
    ghost_south = jnp.where(y_place == 0, along_y, 0.0)
    ghost_north = jnp.where(y_place == side_cells - 1, along_y, 0.0)
    diagonal = (
        face_west
        + face_east
        + face_south
        + face_north
        + face_below
        + face_above
        + ghost_west
        + ghost_east
        + ghost_south
        + ghost_north
        + MASS_SHARE * (along_x + along_y + across_ply)
        + (1.0 - mask_flat)
    )
    return (
        face_west,
        face_east,
        face_south,
        face_north,
        face_below,
        face_above,
        ghost_west,
        ghost_east,
        ghost_south,
        ghost_north,
        diagonal,
        mask_flat,
    )


def operate_flat(field_in, coeffs, side_cells):
    face_west, face_east, face_south, face_north, face_below, face_above = coeffs[:6]
    diagonal = coeffs[10]
    beside = (
        face_west * jnp.roll(field_in, 1, axis=2)
        + face_east * jnp.roll(field_in, -1, axis=2)
        + face_south * jnp.roll(field_in, 1, axis=3)
        + face_north * jnp.roll(field_in, -1, axis=3)
        + face_below * jnp.roll(field_in, side_cells, axis=3)
        + face_above * jnp.roll(field_in, -side_cells, axis=3)
    )
    return diagonal * field_in - beside


def solve_cells(source, knockdown, orient, active, ghosts):
    case_count, sub_count, side_x, flat_width = source.shape
    ply_count = orient.shape[1]
    side_cells = flat_width // ply_count
    coeffs = flat_coeffs(knockdown.astype(jnp.float32), orient, active, side_cells)
    ghost_west, ghost_east, ghost_south, ghost_north, diagonal, mask_flat = coeffs[6:]
    value_west = ghosts[:, :, :, 0:side_cells].reshape(case_count, sub_count, 1, flat_width)
    value_east = ghosts[:, :, :, side_cells : 2 * side_cells].reshape(
        case_count, sub_count, 1, flat_width
    )
    value_south = jnp.repeat(
        jnp.swapaxes(ghosts[:, :, :, 2 * side_cells : 3 * side_cells], 2, 3), side_cells, axis=3
    )
    value_north = jnp.repeat(
        jnp.swapaxes(ghosts[:, :, :, 3 * side_cells :], 2, 3), side_cells, axis=3
    )
    field_cells = source.astype(jnp.float32)
    residual = (
        mask_flat * field_cells
        + ghost_west * value_west
        + ghost_east * value_east
        + ghost_south * value_south
        + ghost_north * value_north
    )
    adjoint = jnp.zeros_like(residual)
    sigma_ratio = CHEB_CENTER / CHEB_HALF
    for sweep_index in range(SWEEPS):
        rho_now = 1.0 / sigma_ratio
        direction = residual / (CHEB_CENTER * diagonal)
        for step_index in range(STEPS):
            adjoint = adjoint + direction
            if not (sweep_index + 1 == SWEEPS and step_index + 1 == STEPS):
                residual = residual - operate_flat(direction, coeffs, side_cells)
            if step_index + 1 < STEPS:
                rho_next = 1.0 / (2.0 * sigma_ratio - rho_now)
                direction = rho_next * rho_now * direction + 2.0 * rho_next / CHEB_HALF * (
                    residual / diagonal
                )
                rho_now = rho_next
    force_west = jnp.sum(ghost_west * (value_west - adjoint), axis=2).reshape(
        case_count, sub_count, ply_count, side_cells
    )
    force_east = jnp.sum(ghost_east * (value_east - adjoint), axis=2).reshape(
        case_count, sub_count, ply_count, side_cells
    )
    south_term = (ghost_south * (value_south - adjoint)).reshape(
        case_count, sub_count, side_x, ply_count, side_cells
    )
    north_term = (ghost_north * (value_north - adjoint)).reshape(
        case_count, sub_count, side_x, ply_count, side_cells
    )
    force_south = jnp.swapaxes(jnp.sum(south_term, axis=4), 2, 3)
    force_north = jnp.swapaxes(jnp.sum(north_term, axis=4), 2, 3)
    forces = jnp.concatenate([force_west, force_east, force_south, force_north], axis=3)
    return (adjoint, forces)


def per_device(shell_state, source, knockdown, orient, active, point_owner, owner_nodes):
    case_count, sub_local, side_x, flat_width = source.shape
    ply_count = orient.shape[1]
    node_local = shell_state.shape[2]
    groups = lax.axis_size("grp")
    tile_count = lax.axis_size("sub")
    devices = groups * tile_count
    slot_depth = owner_nodes.shape[2]
    slot_total = devices * slot_depth
    boundary_width = point_owner.shape[1]
    row_count = sub_local * boundary_width
    node_table = owner_nodes[0]
    live_slot = node_table >= 0
    picked = jnp.where(
        live_slot[None, None], shell_state[:, :, jnp.where(live_slot, node_table, 0)], 0.0
    )
    owners = point_owner.reshape(row_count)
    owner_hit = (owners[:, None] == jnp.arange(devices, dtype=jnp.int32)[None, :]).astype(jnp.int32)
    slot_rank = jnp.sum((jnp.cumsum(owner_hit, axis=0) - owner_hit) * owner_hit, axis=1)
    slot_index = owners * slot_depth + slot_rank
    slot_source = (
        jnp.full((slot_total,), row_count, jnp.int32)
        .at[slot_index]
        .set(jnp.arange(row_count, dtype=jnp.int32))
    )
    arrived = lax.all_to_all(
        picked.reshape(case_count, ply_count, slot_total),
        ("grp", "sub"),
        split_axis=2,
        concat_axis=2,
        tiled=True,
    )
    values = arrived[:, :, slot_index]
    ghosts = jnp.transpose(
        values.reshape(case_count, ply_count, sub_local, boundary_width), (0, 2, 1, 3)
    )

    def solve_one(sub_index):
        sub_source = lax.dynamic_slice_in_dim(source, sub_index, 1, 1)
        sub_knock = lax.dynamic_slice_in_dim(knockdown, sub_index, 1, 0)
        sub_orient = lax.dynamic_slice_in_dim(orient, sub_index, 1, 0)
        sub_active = lax.dynamic_slice_in_dim(active, sub_index, 1, 0)
        sub_ghosts = lax.dynamic_slice_in_dim(ghosts, sub_index, 1, 1)
        return solve_cells(sub_source, sub_knock, sub_orient, sub_active, sub_ghosts)

    adjoint, forces = lax.map(solve_one, jnp.arange(sub_local))
    adjoint = jnp.moveaxis(adjoint[:, :, 0], 0, 1)
    force_rows = jnp.transpose(forces[:, :, 0], (0, 2, 3, 1)).reshape(
        sub_local * boundary_width, case_count * ply_count
    )
    force_rows = jnp.transpose(forces[:, :, 0], (0, 3, 1, 2)).reshape(
        row_count, case_count * ply_count
    )
    padded_rows = jnp.concatenate(
        [force_rows, jnp.zeros((1, case_count * ply_count), jnp.float32)], axis=0
    )
    outbound = padded_rows[slot_source].T.reshape(case_count, ply_count, slot_total)
    returned = lax.all_to_all(outbound, ("grp", "sub"), split_axis=2, concat_axis=2, tiled=True)
    returned_rows = returned.reshape(case_count * ply_count, slot_total).T
    target = jnp.where(live_slot, node_table, node_local).reshape(slot_total)
    node_rows = (
        jnp.zeros((node_local, case_count * ply_count), jnp.float32)
        .at[target]
        .add(returned_rows, mode="drop")
    )
    shell_force = node_rows.T.reshape(case_count, ply_count, node_local)
    return (adjoint, shell_force)


def solution(mesh):
    in_specs = (
        P(None, None, ("grp", "sub")),
        P(None, ("grp", "sub"), None, None),
        P(("grp", "sub"), None, None),
        P(("grp", "sub"), None),
        P(("grp", "sub")),
        P(("grp", "sub"), None),
        P(("grp", "sub"), None, None),
    )
    out_specs = (P(None, ("grp", "sub"), None, None), P(None, None, ("grp", "sub")))
    return jax.shard_map(
        per_device, mesh=mesh, in_specs=in_specs, out_specs=out_specs, check_vma=False
    )
```

profile of v0, /device:TPU:0, one launch (start us, length us, event | category | flops | bytes accessed | tf_op | source)
XLA Modules:
  0.0 206.3 jit_solution(701925207366598028)
XLA Ops:
  0.6 0.7 compare_select_fusion.2
  1.4 0.7 broadcast_compare_fusion
  2.1 10.7 %copy.32 = f32[2,48,8192]{1,0,2:T(2,128)} copy(f32[2,48,8192]{2,1,0:T(8,128)} %param.9) | data formatting | bytes 6291456 | tf_op args[0]
  12.9 6.9 %gather_fusion = f32[1024,2,48]{2,1,0:T(2,128)S(1)} fusion(f32[2,48,8192]{1,0,2:T(2,128)} %copy.32, s32[1024]{0:T(1024)S(1)} %broadcast_clamp_fusion), kind=kCustom, calls=%fused_computation | custom fusion | bytes 790528 | tf_op jit(solution)/shard_map/gather | solution.py:174
  19.8 1.0 copy.47
  20.8 0.9 copy.48
  21.8 3.7 %bitcast_select_fusion = f32[2,48,1024]{1,0,2:T(2,128)S(1)} fusion(f32[2,48,32,32]{1,0,3,2:T(2,128)S(1)} %copy.48, pred[1024]{0:T(1024)(128)(4,1)S(1)} %ge.30), kind=kLoop, calls=%fused_computation.174 | loop fusion | flops 98304 | bytes 787456 | tf_op jit(solution)/shard_map/jit(_where)/select_n | solution.py:173
  25.5 2.6 %reshape.1631 = f32[32,1,3072]{2,1,0:T(1,128)} reshape(f32[1024,2,48]{2,1,0:T(2,128)S(1)} %bitcast.161) | data formatting | bytes 786432
  28.1 7.3 %all-to-all-start = ((f32[32,1,3072]{2,1,0:T(1,128)}), f32[32,1,3072]{2,1,0:T(1,128)S(1)}, u32[]{:S(2)}, u32[]{:S(2)}) async-start(f32[32,1,3072]{2,1,0:T(1,128)} %reshape.1631), calls=%async_computation | async-start | bytes 786432 | tf_op jit(solution)/shard_map/all_to_all | solution.py:185
  35.6 1.2 reduce-window.6
  37.2 2.6 %scatter_custom_fusion = s32[1024]{0:T(1024)S(1)} fusion(s32[512]{0:T(512)S(1)} %bitcast.171, s32[512]{0:T(512)S(1)} %iota.82, s32[]{:T(128)} %constant.156.clone.1), kind=kCustom, calls=%fused_computation.194 | custom fusion | bytes 4100 | tf_op jit(solution)/shard_map/scatter | solution.py:183
  39.9 9.1 %all-to-all-done = f32[32,1,3072]{2,1,0:T(1,128)S(1)} async-done(((f32[32,1,3072]{2,1,0:T(1,128)}), f32[32,1,3072]{2,1,0:T(1,128)S(1)}, u32[]{:S(2)}, u32[]{:S(2)}) %all-to-all-start) | async-done | bytes 393248 | tf_op jit(solution)/shard_map/all_to_all | solution.py:185
  49.5 1.5 reduce.18
  51.0 1.6 reshape.1632
  52.6 2.1 %gather_fusion.1 = f32[512,2,48]{2,1,0:T(2,128)S(1)} fusion(f32[2,48,1024]{1,0,2:T(2,128)S(1)} %bitcast.168, s32[1024]{0:T(1024)S(1)} %pad_clamp_fusion), kind=kCustom, calls=%fused_computation.1 | custom fusion | bytes 395264 | tf_op jit(solution)/shard_map/gather | solution.py:192
  55.0 111.0 %while.14 = (s32[]{:T(128)}, f32[8,2,1,16,768]{4,3,0,1,2:T(8,128)}, f32[8,2,1,48,64]{3,4,1,2,0:T(8,128)S(1)}, s32[8]{0:T(128)S(1)}, s32[8]{0:T(128)S(1)}, /*inde...) while((s32[]{:T(128)}, f32[8,2,1,16,768]{4,3,0,1,2:T(8,128)}, ...), condition=%wide.region_8.9_spmd, body=%wide.region_3.8_spmd.sunk | while | flops 5484184 | bytes 18067664 | solution.py:205
  58.1 1.4 fusion.186
  63.0 0.9 broadcast_divide_fusion.6
  68.2 0.7 bitcast_dynamic-update-slice_fusion.2
  72.0 1.4 fusion.186
  76.9 0.9 broadcast_divide_fusion.6
  82.1 0.7 bitcast_dynamic-update-slice_fusion.2
  85.8 1.4 fusion.186
  90.8 0.9 broadcast_divide_fusion.6
  95.9 0.7 bitcast_dynamic-update-slice_fusion.2
  99.7 1.4 fusion.186
  104.6 0.9 broadcast_divide_fusion.6
  109.8 0.7 bitcast_dynamic-update-slice_fusion.2
  113.6 1.4 fusion.186
  118.5 0.9 broadcast_divide_fusion.6
  123.7 0.7 bitcast_dynamic-update-slice_fusion.2
  127.4 1.4 fusion.186
  132.4 0.9 broadcast_divide_fusion.6
  137.5 0.7 bitcast_dynamic-update-slice_fusion.2
  141.3 1.4 fusion.186
  146.2 0.9 broadcast_divide_fusion.6
  151.4 0.7 bitcast_dynamic-update-slice_fusion.2
  155.2 1.4 fusion.186
  160.1 0.9 broadcast_divide_fusion.6
  165.3 0.7 bitcast_dynamic-update-slice_fusion.2
  166.7 2.8 %gather_fusion.2 = f32[1024,96]{1,0:T(8,128)S(1)} fusion(f32[513,96]{1,0:T(8,128)S(1)} %concatenate.543, s32[1024]{0:T(1024)S(1)} %fusion.100), kind=kCustom, calls=%fused_computation.2 | custom fusion | bytes 790528 | tf_op jit(solution)/shard_map/gather | solution.py:216
  170.2 2.6 %reshape.1633 = f32[32,1,3072]{2,1,0:T(1,128)} reshape(f32[1024,2,48]{2,1,0:T(2,128)S(1)} %bitcast.159) | data formatting | bytes 786432
  172.8 2.8 %all-to-all-start.1 = ((f32[32,1,3072]{2,1,0:T(1,128)}), f32[32,1,3072]{2,1,0:T(1,128)S(1)}, u32[]{:S(2)}, u32[]{:S(2)}) async-start(f32[32,1,3072]{2,1,0:T(1,128)} %reshape.1633), calls=%async_computation.1 | async-start | bytes 786432 | tf_op jit(solution)/shard_map/all_to_all | solution.py:217
  175.7 13.2 %all-to-all-done.1 = f32[32,1,3072]{2,1,0:T(1,128)S(1)} async-done(((f32[32,1,3072]{2,1,0:T(1,128)}), f32[32,1,3072]{2,1,0:T(1,128)S(1)}, u32[]{:S(2)}, u32[]{:S(2)}) %all-to-all-start.1) | async-done | bytes 393248 | tf_op jit(solution)/shard_map/all_to_all | solution.py:217
  189.0 1.5 reduce.19
  190.5 1.7 reshape.1634
  192.8 8.2 %scatter_custom_fusion.1 = f32[8192,96]{1,0:T(8,128)} fusion(s32[1024]{0:T(1024)S(1)} %bitcast.174, f32[1024,96]{1,0:T(8,128)S(1)} %copy.45, f32[]{:T(128)} %constant.152.clone.1), kind=kCustom, calls=%fused_computation.172 | custom fusion | flops 98304 | bytes 3145732 | tf_op jit(solution)/shard_map/scatter-add | solution.py:223
  201.0 5.3 %copy.46 = f32[96,8192]{1,0:T(8,128)} copy(f32[96,8192]{0,1:T(8,128)} %bitcast.155) | data formatting | bytes 6291456 | tf_op jit(solution)/shard_map/transpose | solution.py:225
  (654 shorter events, 73.5 us)
Async XLA Ops:
  19.8 15.6 %copy-start.2 = (s32[8,64]{1,0:T(8,128)S(1)}, s32[8,64]{1,0:T(8,128)}, u32[]{:S(2)}) copy-start(s32[8,64]{1,0:T(8,128)} %param.14) | copy-start | bytes 6148
  21.7 33.3 %copy-start = (bf16[8,16,768]{2,1,0:T(8,128)(2,1)S(1)}, bf16[8,16,768]{2,1,0:T(8,128)(2,1)}, u32[]{:S(2)}) copy-start(bf16[8,16,768]{2,1,0:T(8,128)(2,1)} %param.11) | copy-start | bytes 589828
  21.7 33.3 %copy-start.3 = (s32[8]{0:T(128)S(1)}, s32[8]{0:T(128)}, u32[]{:S(2)}) copy-start(s32[8]{0:T(128)} %param.13) | copy-start | bytes 100
  28.1 20.8 %all-to-all-start = ((f32[32,1,3072]{2,1,0:T(1,128)}), f32[32,1,3072]{2,1,0:T(1,128)S(1)}, u32[]{:S(2)}, u32[]{:S(2)}) async-start(f32[32,1,3072]{2,1,0:T(1,128)} %reshape.1631), calls=%async_computation | async-start | bytes 786432 | tf_op jit(solution)/shard_map/all_to_all | solution.py:185
  166.7 9.0 %copy-start.1 = (s32[1,32,32]{2,1,0:T(8,128)S(1)}, s32[1,32,32]{2,1,0:T(8,128)}, u32[]{:S(2)}) copy-start(s32[1,32,32]{2,1,0:T(8,128)} %param.15) | copy-start | bytes 12292
  172.8 16.1 %all-to-all-start.1 = ((f32[32,1,3072]{2,1,0:T(1,128)}), f32[32,1,3072]{2,1,0:T(1,128)S(1)}, u32[]{:S(2)}, u32[]{:S(2)}) async-start(f32[32,1,3072]{2,1,0:T(1,128)} %reshape.1633), calls=%async_computation.1 | async-start | bytes 786432 | tf_op jit(solution)/shard_map/all_to_all | solution.py:217
where the time goes:
time: 208 us; the launch traced here: 206 us
  local copies, waits for them, and re-layouts  98.7 us (47%)
  other arithmetic  56.3 us (27%)
  waiting for transfers between devices  22.3 us (11%)
  loops' own time  18 us (9%)
  starting transfers between devices  10.1 us (5%)
    unnamed x13, local copies, waits for them, and re-layouts  19.2 us
    another operation x1, loops' own time, per_device(): adjoint, forces = lax.map(solve_one, jnp.arange(sub_local))  18 us
    all_to_all x1, waiting for transfers between devices, per_device(): lax.all_to_all(outbound, ('grp', 'sub'), split_axis=2, concat_axis=2, til...  13.2 us
    mul x8, other arithmetic, flat_coeffs(): (FIBER_COND * (1.0 - cos_square) + TRANSVERSE * cos_square) * active_mask  11.1 us
    div x32, other arithmetic, solve_cells(): direction = residual / (CHEB_CENTER * diagonal)  10.9 us
    all_to_all x1, waiting for transfers between devices, per_device(): lax.all_to_all(picked.reshape(case_count, ply_count, slot_total), ('grp',...  9.06 us
    gather x3, local copies, waits for them, and re-layouts, per_device(): shell_state[:, :, jnp.where(live_slot, node_table, 0)]  8.76 us
    scatter-add x1, other arithmetic, per_device(): node_rows = jnp.zeros((node_local, case_count * ply_count), jnp.float32)....  8.18 us
  transfers between devices with their start and end apart: 2, of which 2 were waited for; matrix products, arithmetic and copies ran while one was open for 2% of the time, Pallas kernels for 0%

commit v1 on v0

--- a/solution.py
+++ b/solution.py
@@ -12,6 +12,12 @@
 MASS_SHARE = 0.05
 CHEB_CENTER = 1.02
 CHEB_HALF = 0.98
+
+
+def trade_parts(x, axis, split, join):
+    cells = jnp.split(x, lax.axis_size(axis), axis=split)
+    received = lax.all_to_all(jnp.stack(cells), axis, 0, 0)
+    return jnp.concatenate(received, axis=join)
 
 
 def face_mean(lower_side, upper_side):
@@ -214,7 +220,7 @@
         [force_rows, jnp.zeros((1, case_count * ply_count), jnp.float32)], axis=0
     )
     outbound = padded_rows[slot_source].T.reshape(case_count, ply_count, slot_total)
-    returned = lax.all_to_all(outbound, ("grp", "sub"), split_axis=2, concat_axis=2, tiled=True)
+    returned = trade_parts(outbound, ("grp", "sub"), 2, 2)
     returned_rows = returned.reshape(case_count * ply_count, slot_total).T
     target = jnp.where(live_slot, node_table, node_local).reshape(slot_total)
     node_rows = (

time: 208 us -> 215 us (1.034)
  waiting for transfers between devices: 22.3 us -> 26.6 us
  local copies, waits for them, and re-layouts: 98.7 us -> 101 us
    all_to_all x1, waiting for transfers between devices: 9.06 us -> 13.3 us  [per_device(): lax.all_to_all(picked.reshape(case_count, ply_count, slot_total), ('grp',...]
    unnamed x13 -> x42, local copies, waits for them, and re-layouts: 19.2 us -> 19.1 us
  transfers between devices with their start and end apart: 2 -> 2, of which waited for: 2 -> 2; matrix products, arithmetic and copies ran while one was open for 2% -> 0% of each run, Pallas kernels for 0% -> 0%
where the time goes in v1:
time: 215 us; the launch traced here: 213 us
  local copies, waits for them, and re-layouts  101 us (47%)
  other arithmetic  56.5 us (26%)
  waiting for transfers between devices  26.6 us (12%)
  loops' own time  18.1 us (8%)
  starting transfers between devices  10.3 us (5%)
    unnamed x42, local copies, waits for them, and re-layouts  19.1 us
    another operation x1, loops' own time, per_device(): adjoint, forces = lax.map(solve_one, jnp.arange(sub_local))  18.1 us
    all_to_all x1, waiting for transfers between devices, per_device(): lax.all_to_all(picked.reshape(case_count, ply_count, slot_total), ('grp',...  13.3 us
    all_to_all x1, waiting for transfers between devices, trade_parts(): received = lax.all_to_all(jnp.stack(cells), axis, 0, 0)  13.2 us
    mul x8, other arithmetic, flat_coeffs(): (FIBER_COND * (1.0 - cos_square) + TRANSVERSE * cos_square) * active_mask  11.1 us
    div x32, other arithmetic, solve_cells(): direction = residual / (CHEB_CENTER * diagonal)  10.7 us
    gather x3, local copies, waits for them, and re-layouts, per_device(): shell_state[:, :, jnp.where(live_slot, node_table, 0)]  8.76 us
    scatter-add x1, other arithmetic, per_device(): node_rows = jnp.zeros((node_local, case_count * ply_count), jnp.float32)....  8.21 us
  transfers between devices with their start and end apart: 2, of which 2 were waited for; matrix products, arithmetic and copies ran while one was open for 0% of the time, Pallas kernels for 0%

profile of v1, /device:TPU:0, one launch (start us, length us, event | category | flops | bytes accessed | tf_op | source)
XLA Modules:
  0.0 212.9 jit_solution(11566306725449504400)
XLA Ops:
  0.6 0.8 eq.111
  1.4 0.8 eq.107
  2.2 0.7 broadcast_multiply_fusion.1
  2.8 0.7 compare_select_fusion.2
  3.6 0.7 broadcast_compare_fusion
  4.3 1.2 reduce-window.6
  5.9 10.7 %copy.32 = f32[2,48,8192]{1,0,2:T(2,128)} copy(f32[2,48,8192]{2,1,0:T(8,128)} %param.9) | data formatting | bytes 6291456 | tf_op args[0]
  16.7 2.4 %scatter_custom_fusion = s32[1024]{0:T(1024)S(1)} fusion(s32[512]{0:T(512)S(1)} %bitcast.333, s32[512]{0:T(512)S(1)} %iota.82, s32[]{:T(128)} %constant.156.clone.1), kind=kCustom, calls=%fused_computation.259 | custom fusion | bytes 4100 | tf_op jit(solution)/shard_map/scatter | solution.py:189
  19.2 6.9 %gather_fusion = f32[1024,2,48]{2,1,0:T(2,128)S(1)} fusion(f32[2,48,8192]{1,0,2:T(2,128)} %copy.32, s32[1024]{0:T(1024)S(1)} %get-tuple-element.290), kind=kCustom, calls=%fused_computation | custom fusion | bytes 790528 | tf_op jit(solution)/shard_map/gather | solution.py:180
  26.1 1.0 copy.46
  27.1 0.9 copy.47
  28.1 3.7 %bitcast_select_fusion = f32[2,48,1024]{1,0,2:T(2,128)S(1)} fusion(f32[2,48,32,32]{1,0,3,2:T(2,128)S(1)} %copy.47, pred[1024]{0:T(1024)(128)(4,1)S(1)} %ge.30), kind=kLoop, calls=%fused_computation.174 | loop fusion | flops 98304 | bytes 787456 | tf_op jit(solution)/shard_map/jit(_where)/select_n | solution.py:179
  31.8 2.6 %reshape.1631 = f32[32,1,3072]{2,1,0:T(1,128)} reshape(f32[1024,2,48]{2,1,0:T(2,128)S(1)} %bitcast.325) | data formatting | bytes 786432
  34.4 7.5 %all-to-all-start = ((f32[32,1,3072]{2,1,0:T(1,128)}), f32[32,1,3072]{2,1,0:T(1,128)S(1)}, u32[]{:S(2)}, u32[]{:S(2)}) async-start(f32[32,1,3072]{2,1,0:T(1,128)} %reshape.1631), calls=%async_computation | async-start | bytes 786432 | tf_op jit(solution)/shard_map/all_to_all | solution.py:191
  41.9 13.3 %all-to-all-done = f32[32,1,3072]{2,1,0:T(1,128)S(1)} async-done(((f32[32,1,3072]{2,1,0:T(1,128)}), f32[32,1,3072]{2,1,0:T(1,128)S(1)}, u32[]{:S(2)}, u32[]{:S(2)}) %all-to-all-start) | async-done | bytes 393248 | tf_op jit(solution)/shard_map/all_to_all | solution.py:191
  55.8 1.5 reduce.18
  57.3 1.6 reshape.1632
  58.9 2.1 gather_fusion.1
  61.2 110.5 %while.14 = (s32[]{:T(128)}, f32[8,2,1,16,768]{4,3,0,1,2:T(8,128)}, f32[8,2,1,48,64]{3,4,1,2,0:T(8,128)S(1)}, s32[8]{0:T(128)S(1)}, s32[8]{0:T(128)S(1)}, /*inde...) while((s32[]{:T(128)}, f32[8,2,1,16,768]{4,3,0,1,2:T(8,128)}, ...), condition=%wide.region_8.9_spmd, body=%wide.region_3.8_spmd.sunk | while | flops 5484184 | bytes 18067664 | solution.py:211
  64.4 1.4 fusion.187
  69.3 0.9 broadcast_divide_fusion.6
  74.4 0.7 bitcast_dynamic-update-slice_fusion.2
  78.2 1.4 fusion.187
  83.1 0.9 broadcast_divide_fusion.6
  88.2 0.7 bitcast_dynamic-update-slice_fusion.2
  92.0 1.4 fusion.187
  96.9 0.9 broadcast_divide_fusion.6
  102.0 0.7 bitcast_dynamic-update-slice_fusion.2
  105.8 1.4 fusion.187
  110.7 0.9 broadcast_divide_fusion.6
  115.8 0.7 bitcast_dynamic-update-slice_fusion.2
  119.6 1.4 fusion.187
  124.5 0.9 broadcast_divide_fusion.6
  129.6 0.7 bitcast_dynamic-update-slice_fusion.2
  133.4 1.4 fusion.187
  138.4 0.9 broadcast_divide_fusion.6
  147.2 1.4 fusion.187
  152.2 0.9 broadcast_divide_fusion.6
  161.0 1.4 fusion.187
  166.0 0.9 broadcast_divide_fusion.6
  172.5 2.8 %gather_fusion.2 = f32[1024,96]{1,0:T(8,128)S(1)} fusion(f32[513,96]{1,0:T(8,128)S(1)} %concatenate.543, s32[1024]{0:T(1024)S(1)} %get-tuple-element.289), kind=kCustom, calls=%fused_computation.2 | custom fusion | bytes 790528 | tf_op jit(solution)/shard_map/gather | solution.py:222
  178.0 1.7 reshape.1633
  179.8 2.8 %all-to-all-start.1 = ((f32[32,1,3072]{2,1,0:T(1,128)}), f32[32,1,3072]{2,1,0:T(1,128)S(1)}, u32[]{:S(2)}, u32[]{:S(2)}) async-start(f32[32,1,3072]{2,1,0:T(1,128)} %reshape.1633), calls=%async_computation.1 | async-start | bytes 786432 | tf_op jit(solution)/shard_map/all_to_all | solution.py:19
  182.7 13.2 %all-to-all-done.1 = f32[32,1,3072]{2,1,0:T(1,128)S(1)} async-done(((f32[32,1,3072]{2,1,0:T(1,128)}), f32[32,1,3072]{2,1,0:T(1,128)S(1)}, u32[]{:S(2)}, u32[]{:S(2)}) %all-to-all-start.1) | async-done | bytes 393248 | tf_op jit(solution)/shard_map/all_to_all | solution.py:19
  195.9 1.5 reduce.19
  198.0 0.8 copy.44
  199.4 8.2 %scatter_custom_fusion.1 = f32[8192,96]{1,0:T(8,128)} fusion(s32[1024]{0:T(1024)S(1)} %bitcast.336, f32[]{:T(128)} %constant.152.clone.1, f32[96,1024]{0,1:T(8,128)S(1)} %reshape_reshape.3), kind=kCustom, calls=%fused_computation.172 | custom fusion | flops 98304 | bytes 3670020 | tf_op jit(solution)/shard_map/scatter-add | solution.py:229
  207.6 5.3 %copy.45 = f32[96,8192]{1,0:T(8,128)} copy(f32[96,8192]{0,1:T(8,128)} %bitcast.288) | data formatting | bytes 6291456 | tf_op jit(solution)/shard_map/transpose | solution.py:231
  (684 shorter events, 77.2 us)
Async XLA Ops:
  34.4 20.8 %all-to-all-start = ((f32[32,1,3072]{2,1,0:T(1,128)}), f32[32,1,3072]{2,1,0:T(1,128)S(1)}, u32[]{:S(2)}, u32[]{:S(2)}) async-start(f32[32,1,3072]{2,1,0:T(1,128)} %reshape.1631), calls=%async_computation | async-start | bytes 786432 | tf_op jit(solution)/shard_map/all_to_all | solution.py:191
  57.3 4.0 %copy-start = (bf16[8,16,768]{2,1,0:T(8,128)(2,1)S(1)}, bf16[8,16,768]{2,1,0:T(8,128)(2,1)}, u32[]{:S(2)}) copy-start(bf16[8,16,768]{2,1,0:T(8,128)(2,1)} %param.11) | copy-start | bytes 589828
  57.3 4.0 %copy-start.2 = (s32[8]{0:T(128)S(1)}, s32[8]{0:T(128)}, u32[]{:S(2)}) copy-start(s32[8]{0:T(128)} %param.13) | copy-start | bytes 100
  178.0 4.6 %copy-start.1 = (s32[1,32,32]{2,1,0:T(8,128)S(1)}, s32[1,32,32]{2,1,0:T(8,128)}, u32[]{:S(2)}) copy-start(s32[1,32,32]{2,1,0:T(8,128)} %param.15) | copy-start | bytes 12292
  179.8 16.1 %all-to-all-start.1 = ((f32[32,1,3072]{2,1,0:T(1,128)}), f32[32,1,3072]{2,1,0:T(1,128)S(1)}, u32[]{:S(2)}, u32[]{:S(2)}) async-start(f32[32,1,3072]{2,1,0:T(1,128)} %reshape.1633), calls=%async_computation.1 | async-start | bytes 786432 | tf_op jit(solution)/shard_map/all_to_all | solution.py:19
